TPU v7x, 32 devices: a whole 2x2x4 slice. The times are simulated.
32 devices in a mesh: dp: 16 (over z, x, core), tensor: 2 (over y).
Axes of the slice: x: 2, y: 2, z: 4, core: 2. Of those that a mesh axis runs over, the one named last changes fastest.
Arguments:
- inputs: bfloat16 [32768, 1024], P('dp'), may hold values from -6 to 6
- cotangent: bfloat16 [32768, 1024], P('dp'), may hold values from -6 to 6
- segment_ids: int32 [16, 2048], P('dp'), may hold values from 0 to 7, never falling along the last dimension, each value on 1 to 1024 neighbouring positions
- w_qkv: float32 [3, 1024, 1024], P(None, 'dp', 'tensor'), may hold values from -0.1875 to 0.1875
- w_out: float32 [1024, 1024], P('tensor', 'dp'), may hold values from -1.5 to 1.5
- w_fc1: float32 [1024, 4096], P('dp', 'tensor'), may hold values from -0.1875 to 0.1875
- w_fc2: float32 [4096, 1024], P('tensor', 'dp'), may hold values from -0.09375 to 0.09375
- norm_gain: float32 [4, 1024], replicated, may hold values from 0.5 to 1.5
- norm_bias: float32 [4, 1024], replicated, may hold values from -1.8 to 1.8
- head_bias: float32 [2, 1024], replicated, may hold values from -3 to 3
- out_bias: float32 [2, 1024], replicated, may hold values from -1.2 to 1.2
- fc1_bias: float32 [4096], replicated, may hold values from -1.8 to 1.8
Outputs:
- output: bfloat16 [32768, 1024], P(('dp', 'tensor'))
- d_inputs: bfloat16 [32768, 1024], P(('dp', 'tensor'))
- grad_qkv: float32 [3, 1024, 1024], P(None, 'dp', 'tensor')
- grad_out: float32 [1024, 1024], P('tensor', 'dp')
- grad_fc1: float32 [1024, 4096], P('dp', 'tensor')
- grad_fc2: float32 [4096, 1024], P('tensor', 'dp')
- grad_norm_gain: float32 [4, 1024], replicated
- grad_norm_bias: float32 [4, 1024], replicated
- grad_head_bias: float32 [2, 1024], replicated
- grad_out_bias: float32 [2, 1024], replicated
- grad_fc1_bias: float32 [4096], replicated
Inputs may be any that keep to these rules, and one draw needn't show every extreme that they name: `segment_ids`: in each packed sequence the segment numbers start at 0, never fall, and every number up to the sequence's largest appears; a segment is a document or the padding at the sequence's end. A segment has at most 1024 tokens, and some segment has exactly that many.
All inputs are finite; a program needn't handle non-finite values.
Results may differ from a plain program's by a relative error of at most 0.02.
Values may be sent and summed in bfloat16 or wider, within the bound.
No kernel may reach another device: no remote copies, remote signals or barrier semaphores. Data moves between devices by JAX's collectives and lax.ppermute only.
A program may use at most 512 MiB of HBM per device.

v0:
```python
from functools import partial
import jax
import jax.numpy as jnp
from jax import lax
from jax.sharding import PartitionSpec as P

HD = 64
eps_norm = 1e-05
query_scale = 0.00390625
relax_alpha = 32.0
masked_score = -1000000000.0


def layer_norm(values, gain_row, shift_row):
    row_mean = jnp.mean(values, axis=-1, keepdims=True)
    centered = values - row_mean
    variance = jnp.mean(centered * centered, axis=-1, keepdims=True)
    return centered * lax.rsqrt(variance + eps_norm) * gain_row + shift_row


def norm_back(values, gain_row, shift_row, grad_rows, own_start, own_count):
    pull_back = jax.vjp(lambda inner_values: layer_norm(inner_values, gain_row, shift_row), values)[
        1
    ]
    d_values = pull_back(grad_rows)[0]
    own_values = lax.dynamic_slice_in_dim(values, own_start, own_count, 0)
    own_grad = lax.dynamic_slice_in_dim(grad_rows, own_start, own_count, 0)
    row_mean = jnp.mean(own_values, axis=-1, keepdims=True)
    centered = own_values - row_mean
    variance = jnp.mean(centered * centered, axis=-1, keepdims=True)
    normed = centered * lax.rsqrt(variance + eps_norm)
    return (d_values, jnp.sum(normed * own_grad, axis=0), jnp.sum(own_grad, axis=0))


def gelu_tanh(values):
    return jax.nn.gelu(values, approximate=True)


def contract_rows(left_side, right_side):
    return lax.dot_general(
        left_side, right_side, (((0,), (0,)), ((), ())), preferred_element_type=jnp.float32
    )


def contract_cols(left_side, right_side):
    return lax.dot_general(
        left_side, right_side, (((1,), (1,)), ((), ())), preferred_element_type=jnp.float32
    )


def allowed_mask(segment, row_first, block_rows, key_count):
    query_seg = lax.slice_in_dim(segment, row_first, row_first + block_rows)
    query_pos = row_first + jnp.arange(block_rows, dtype=jnp.int32)
    key_pos = jnp.arange(key_count, dtype=jnp.int32)
    return (query_seg[:, None] == segment[None, :key_count]) & (
        key_pos[None, :] <= query_pos[:, None]
    )


def attend_forward(block_rows, packed):
    queries, key_rows, values, segment = packed
    seq_length = queries.shape[0]
    outputs, peak_list, total_list = ([], [], [])
    for row_first in range(0, seq_length, block_rows):
        row_last = row_first + block_rows
        scaled = queries[row_first:row_last] * query_scale
        scores = jnp.einsum(
            "qhd,khd->hqk", scaled, key_rows[:row_last], preferred_element_type=jnp.float32
        )
        allowed = allowed_mask(segment, row_first, block_rows, row_last)
        scores = jnp.where(allowed[None], scores, masked_score)
        row_peak = jnp.max(scores, axis=2, keepdims=True)
        exponent = jnp.exp(relax_alpha * (scores - row_peak))
        row_total = jnp.sum(exponent, axis=2, keepdims=True)
        probability = (exponent / row_total).astype(jnp.bfloat16)
        outputs.append(
            jnp.einsum(
                "hqk,khd->qhd", probability, values[:row_last], preferred_element_type=jnp.float32
            )
        )
        peak_list.append(row_peak)
        total_list.append(row_total)
    return (
        jnp.concatenate(outputs, axis=0).astype(jnp.bfloat16),
        jnp.stack(peak_list),
        jnp.stack(total_list),
    )


def attend_backward(block_rows, packed):
    queries, key_rows, values, grad_rows, segment, peak_list, total_list = packed
    seq_length = queries.shape[0]
    key_accum = jnp.zeros(key_rows.shape, jnp.float32)
    value_accum = jnp.zeros(values.shape, jnp.float32)
    query_parts = []
    for block_index, row_first in enumerate(range(0, seq_length, block_rows)):
        row_last = row_first + block_rows
        scaled = queries[row_first:row_last] * query_scale
        scores = jnp.einsum(
            "qhd,khd->hqk", scaled, key_rows[:row_last], preferred_element_type=jnp.float32
        )
        allowed = allowed_mask(segment, row_first, block_rows, row_last)
        scores = jnp.where(allowed[None], scores, masked_score)
        probability = (
            jnp.exp(relax_alpha * (scores - peak_list[block_index])) / total_list[block_index]
        )
        prob_low = probability.astype(jnp.bfloat16)
        block_grad = grad_rows[row_first:row_last]
        value_accum = value_accum.at[:row_last].add(
            jnp.einsum("hqk,qhd->khd", prob_low, block_grad, preferred_element_type=jnp.float32)
        )
        d_prob = jnp.einsum(
            "qhd,khd->hqk", block_grad, values[:row_last], preferred_element_type=jnp.float32
        )
        d_scores = (
            relax_alpha
            * probability
            * (d_prob - jnp.sum(probability * d_prob, axis=2, keepdims=True))
        )
        d_scores = d_scores.astype(jnp.bfloat16)
        query_parts.append(
            jnp.einsum(
                "hqk,khd->qhd", d_scores, key_rows[:row_last], preferred_element_type=jnp.float32
            )
            * query_scale
        )
        key_accum = key_accum.at[:row_last].add(
            jnp.einsum("hqk,qhd->khd", d_scores, scaled, preferred_element_type=jnp.float32)
        )
    d_queries = jnp.concatenate(query_parts, axis=0).astype(jnp.bfloat16)
    return (d_queries, key_accum.astype(jnp.bfloat16), value_accum.astype(jnp.bfloat16))


def per_device(
    inputs,
    cotangent,
    segment_ids,
    w_qkv,
    w_out,
    w_fc1,
    w_fc2,
    norm_gain,
    norm_bias,
    head_bias,
    out_bias,
    fc1_bias,
):
    tensor_count = lax.axis_size("tensor")
    tensor_rank = lax.axis_index("tensor")
    token_count = inputs.shape[0]
    seq_count, seq_length = segment_ids.shape
    block_rows = min(512, seq_length)
    shard_rows = token_count // tensor_count
    row_start = tensor_rank * shard_rows
    w_attn, w_proj, w_up, w_down = (
        lax.all_gather(w_qkv.astype(jnp.bfloat16), "dp", axis=1, tiled=True),
        lax.all_gather(w_out.astype(jnp.bfloat16), "dp", axis=1, tiled=True),
        lax.all_gather(w_fc1.astype(jnp.bfloat16), "dp", axis=0, tiled=True),
        lax.all_gather(w_fc2.astype(jnp.bfloat16), "dp", axis=1, tiled=True),
    )
    group_width = w_attn.shape[2]
    hidden_width = w_up.shape[1]
    local_heads = group_width // HD
    col_start = tensor_rank * group_width
    hid_start = tensor_rank * hidden_width
    bias_heads = lax.dynamic_slice_in_dim(head_bias, col_start, group_width, 1)
    bias_hidden = lax.dynamic_slice_in_dim(fc1_bias, hid_start, hidden_width, 0)
    inputs_wide = inputs.astype(jnp.float32)
    normed_in = layer_norm(inputs_wide, norm_gain[0], norm_bias[0]).astype(jnp.bfloat16)
    projected = jnp.einsum("td,jdc->jtc", normed_in, w_attn, preferred_element_type=jnp.float32)
    queries = (projected[0] + bias_heads[0]).astype(jnp.bfloat16)
    key_rows = projected[1].astype(jnp.bfloat16)
    values = (projected[2] + bias_heads[1]).astype(jnp.bfloat16)
    head_shape = (seq_count, seq_length, local_heads, HD)
    query_heads = queries.reshape(head_shape)
    key_heads = key_rows.reshape(head_shape)
    value_heads = values.reshape(head_shape)
    attended, peak_list, total_list = lax.map(
        partial(attend_forward, block_rows), (query_heads, key_heads, value_heads, segment_ids)
    )
    attended = attended.reshape(token_count, group_width)
    partial_attn = jnp.dot(attended, w_proj, preferred_element_type=jnp.float32)
    attn_rows = (
        lax.psum(partial_attn.astype(jnp.bfloat16), "tensor").astype(jnp.float32) + out_bias[0]
    )
    resid = inputs_wide + layer_norm(attn_rows, norm_gain[1], norm_bias[1])
    normed_mid = layer_norm(resid, norm_gain[2], norm_bias[2]).astype(jnp.bfloat16)
    pre_act = jnp.dot(normed_mid, w_up, preferred_element_type=jnp.float32) + bias_hidden
    activated = gelu_tanh(pre_act).astype(jnp.bfloat16)
    partial_mlp = jnp.dot(activated, w_down, preferred_element_type=jnp.float32)
    mlp_rows = (
        lax.psum(partial_mlp.astype(jnp.bfloat16), "tensor").astype(jnp.float32) + out_bias[1]
    )
    cot_rows = cotangent.astype(jnp.float32)
    out_rows = resid + layer_norm(mlp_rows, norm_gain[3], norm_bias[3])
    d_mlp, gain_three, shift_three = norm_back(
        mlp_rows, norm_gain[3], norm_bias[3], cot_rows, row_start, shard_rows
    )
    d_mlp_low = d_mlp.astype(jnp.bfloat16)
    bias_mlp = jnp.sum(
        lax.dynamic_slice_in_dim(d_mlp_low, row_start, shard_rows, 0), axis=0, dtype=jnp.float32
    )
    grad_down = contract_rows(activated, d_mlp_low)
    d_act = contract_cols(d_mlp_low, w_down)
    d_pre = jax.vjp(gelu_tanh, pre_act)[1](d_act)[0].astype(jnp.bfloat16)
    grad_up = contract_rows(normed_mid, d_pre)
    grad_hidden = jnp.sum(d_pre, axis=0, dtype=jnp.float32)
    partial_mid = contract_cols(d_pre, w_up)
    d_mid = lax.psum(partial_mid.astype(jnp.bfloat16), "tensor").astype(jnp.float32)
    d_resid_part, gain_two, shift_two = norm_back(
        resid, norm_gain[2], norm_bias[2], d_mid, row_start, shard_rows
    )
    d_resid = cot_rows + d_resid_part
    d_attn, gain_one, shift_one = norm_back(
        attn_rows, norm_gain[1], norm_bias[1], d_resid, row_start, shard_rows
    )
    d_attn_low = d_attn.astype(jnp.bfloat16)
    bias_attn = jnp.sum(
        lax.dynamic_slice_in_dim(d_attn_low, row_start, shard_rows, 0), axis=0, dtype=jnp.float32
    )
    grad_proj = contract_rows(attended, d_attn_low)
    d_attended = contract_cols(d_attn_low, w_proj).astype(jnp.bfloat16)
    d_queries, d_keys, d_values = lax.map(
        partial(attend_backward, block_rows),
        (
            query_heads,
            key_heads,
            value_heads,
            d_attended.reshape(head_shape),
            segment_ids,
            peak_list,
            total_list,
        ),
    )
    d_proj = jnp.stack(
        [
            d_queries.reshape(token_count, group_width),
            d_keys.reshape(token_count, group_width),
            d_values.reshape(token_count, group_width),
        ]
    )
    grad_attn = jnp.einsum("td,jtc->jdc", normed_in, d_proj, preferred_element_type=jnp.float32)
    partial_in = jnp.einsum("jtc,jdc->td", d_proj, w_attn, preferred_element_type=jnp.float32)
    d_in = lax.psum(partial_in.astype(jnp.bfloat16), "tensor").astype(jnp.float32)
    d_input_part, gain_zero, shift_zero = norm_back(
        inputs_wide, norm_gain[0], norm_bias[0], d_in, row_start, shard_rows
    )
    d_inputs = d_resid + d_input_part
    layer_out = lax.dynamic_slice_in_dim(out_rows, row_start, shard_rows, 0)
    d_out_rows = lax.dynamic_slice_in_dim(d_inputs, row_start, shard_rows, 0)
    head_terms = jnp.stack(
        [
            jnp.sum(d_proj[0], axis=0, dtype=jnp.float32),
            jnp.sum(d_proj[2], axis=0, dtype=jnp.float32),
        ]
    )
    head_full = lax.dynamic_update_slice_in_dim(
        jnp.zeros(head_bias.shape, jnp.float32), head_terms, col_start, 1
    )
    hidden_full = lax.dynamic_update_slice_in_dim(
        jnp.zeros(fc1_bias.shape, jnp.float32), grad_hidden, hid_start, 0
    )
    gain_terms = jnp.stack([gain_zero, gain_one, gain_two, gain_three])
    shift_terms = jnp.stack([shift_zero, shift_one, shift_two, shift_three])
    bias_terms = jnp.stack([bias_attn, bias_mlp])
    gain_sum, shift_sum, head_sum, bias_sum, hidden_sum = lax.psum(
        (gain_terms, shift_terms, head_full, bias_terms, hidden_full), ("dp", "tensor")
    )
    grad_qkv, grad_out, grad_fc1, grad_fc2 = (
        lax.psum_scatter(
            grad_attn.astype(jnp.bfloat16), "dp", scatter_dimension=1, tiled=True
        ).astype(jnp.float32),
        lax.psum_scatter(
            grad_proj.astype(jnp.bfloat16), "dp", scatter_dimension=1, tiled=True
        ).astype(jnp.float32),
        lax.psum_scatter(
            grad_up.astype(jnp.bfloat16), "dp", scatter_dimension=0, tiled=True
        ).astype(jnp.float32),
        lax.psum_scatter(
            grad_down.astype(jnp.bfloat16), "dp", scatter_dimension=1, tiled=True
        ).astype(jnp.float32),
    )
    return (
        layer_out.astype(jnp.bfloat16),
        d_out_rows.astype(jnp.bfloat16),
        grad_qkv,
        grad_out,
        grad_fc1,
        grad_fc2,
        gain_sum,
        shift_sum,
        head_sum,
        bias_sum,
        hidden_sum,
    )


def solution(mesh):
    return jax.shard_map(
        per_device,
        mesh=mesh,
        in_specs=(
            P("dp", None),
            P("dp", None),
            P("dp", None),
            P(None, "dp", "tensor"),
            P("tensor", "dp"),
            P("dp", "tensor"),
            P("tensor", "dp"),
            P(),
            P(),
            P(),
            P(),
            P(),
        ),
        out_specs=(
            P(("dp", "tensor"), None),
            P(("dp", "tensor"), None),
            P(None, "dp", "tensor"),
            P("tensor", "dp"),
            P("dp", "tensor"),
            P("tensor", "dp"),
            P(),
            P(),
            P(),
            P(),
            P(),
        ),
        check_vma=False,
    )
```

profile of v0, /device:TPU:1, one launch (start us, length us, event | category | flops | bytes accessed | tf_op | source)
XLA Modules:
  0.0 1505.4 jit_solution(5447794359743557644)
XLA Ops:
  26.9 31.7 %all-gather.5.cloned.1.call-done = bf16[3,1024,512]{2,1,0:T(8,128)(2,1)} async-done(((bf16[3,64,512]{2,1,0:T(8,128)(2,1)}), bf16[3,1024,512]{2,1,0:T(8,128)(2,1)}) %all-gather.5.cloned.1.call-update) | async-done | bytes 3145744 | tf_op jit(solution)/shard_map/all_gather | solution.py:156
  102.3 14.9 fusion.134
  128.7 18.2 %fusion.133 = (f32[8,512]{1,0:T(8,128)S(1)}, f32[8,512,2048]{2,1,0:T(8,128)}) fusion(pred[512,2048]{1,0:T(8,128)(4,1)} %fusion.53, bf16[512,8,64]{0,2,1:T(8,128)(2,1)S(1)} %bitcast.230, bf16[2048,8,64]{0,2,1:T(8,128)(2,1)S(1)} %bitcast.202), kind=kOutput, calls=%fused_computation.236 | convolution fusion | flops 1107298304 | bytes 37240832 | tf_op jit(solution)/shard_map/while/body/eval_jaxpr/sub | solution.py:73
  146.9 15.9 %fusion.99 = bf16[8,64,512]{2,1,0:T(8,128)(2,1)} fusion(f32[2048,8,64]{0,2,1:T(8,128)} %bitcast.223, f32[8,64]{1,0:T(8,128)S(1)} %add.363, f32[8,512,2048]{2,1,0:T(8,128)} %get-tuple-element.304, f32[8,512]{1,0:T(8,128)S(1)} %get-tuple-element.303), kind=kOutput, calls=%fused_computation.170 | convolution fusion | flops 1092878336 | bytes 38291456 | tf_op jit(solution)/shard_map/while/body/eval_jaxpr/hqk,khd->qhd/dot_general | solution.py:77
  180.0 104.7 %all-reduce.11.cloned.1.call-done = bf16[2048,1024]{1,0:T(8,128)(2,1)} async-done(((bf16[2048,1024]{1,0:T(8,128)(2,1)}), bf16[2048,1024]{1,0:T(8,128)(2,1)}) %all-reduce.11.cloned.1.call-update) | async-done | bytes 4194320 | tf_op jit(solution)/shard_map/psum | solution.py:184
  301.1 37.4 %all-gather.9.cloned.1.call-done = bf16[1024,2048]{1,0:T(8,128)(2,1)} async-done(((bf16[64,2048]{1,0:T(8,128)(2,1)}), bf16[1024,2048]{1,0:T(8,128)(2,1)}) %all-gather.9.cloned.1.call-update) | async-done | bytes 4194320 | tf_op jit(solution)/shard_map/all_gather | solution.py:158
  338.5 20.4 %multiply_convert_fusion.3 = (bf16[2048,2048]{1,0:T(8,128)(2,1)}, f32[2048,2048]{1,0:T(8,128)}) fusion(f32[2048]{0:T(1024)S(1)} %dynamic_slice.68, bf16[1024,2048]{1,0:T(8,128)(2,1)} %all-gather.9.cloned.1.call-done, f32[2048,1024]{1,0:T(8,128)} %copy-done, f32[1024]{0:T(1024)S(1)} %bitcast.296, f32[1024]{0:T(1024)S(1)} %bitcast.265, ...), kind=kOutput, calls=%fused_computation.26 | convolution fusion | flops 8642363392 | bytes 37781504 | tf_op jit(solution)/shard_map/dot_general | solution.py:188
  358.9 31.7 %all-gather.11.cloned.1.call-done = bf16[2048,1024]{0,1:T(8,128)(2,1)} async-done(((bf16[2048,64]{0,1:T(8,128)(2,1)}), bf16[2048,1024]{0,1:T(8,128)(2,1)}) %all-gather.11.cloned.1.call-update) | async-done | bytes 4194320 | tf_op jit(solution)/shard_map/all_gather | solution.py:159
  390.6 13.9 convolution_convert_fusion.2
  404.5 106.0 %all-reduce.13.cloned.1.call-done = bf16[2048,1024]{1,0:T(8,128)(2,1)} async-done(((bf16[2048,1024]{1,0:T(8,128)(2,1)}), bf16[2048,1024]{1,0:T(8,128)(2,1)}) %all-reduce.13.cloned.1.call-update) | async-done | bytes 4194320 | tf_op jit(solution)/shard_map/psum | solution.py:192
  530.5 24.9 %convert_reduce_fusion = (f32[2048]{0:T(1024)}, bf16[2048,2048]{1,0:T(8,128)(2,1)S(1)}) fusion(f32[2048,2048]{1,0:T(8,128)} %get-tuple-element.312, f32[2048]{0:T(1024)S(1)} %dynamic_slice.68, bf16[2048,1024]{1,0:T(8,128)(2,1)S(1)} %get-tuple-element.273, bf16[2048,1024]{0,1:T(8,128)(2,1)S(1)} %copy-done.97), kind=kOutput, calls=%fused_computation.23 | convolution fusion | flops 8686401536 | bytes 33570816 | tf_op jit(solution)/shard_map/dot_general | solution.py:46
  569.3 108.0 %all-reduce.15.cloned.1.call-done = bf16[2048,1024]{1,0:T(8,128)(2,1)} async-done(((bf16[2048,1024]{1,0:T(8,128)(2,1)}), bf16[2048,1024]{1,0:T(8,128)(2,1)}) %all-reduce.15.cloned.1.call-update) | async-done | bytes 4194320 | tf_op jit(solution)/shard_map/psum | solution.py:209
  742.0 16.6 %multiply_reduce_fusion.1 = (f32[8,512]{1,0:T(8,128)}, f32[8,512,1536]{2,1,0:T(8,128)}) fusion(f32[8,512,1536]{2,1,0:T(8,128)} %get-tuple-element.306, f32[8,512]{1,0:T(8,128)S(1)} %copy-done.71, bf16[512,8,64]{0,2,1:T(8,128)(2,1)S(1)} %bitcast.244, bf16[1536,8,64]{0,2,1:T(8,128)(2,1)S(1)} %bitcast.237), kind=kOutput, calls=%fused_computation.10 | convolution fusion | flops 824176640 | bytes 52461568 | tf_op jit(solution)/shard_map/while/body/eval_jaxpr/qhd,khd->hqk/dot_general | solution.py:112
  771.3 22.0 %multiply_reduce_fusion = (f32[8,512]{1,0:T(8,128)}, f32[8,512,2048]{2,1,0:T(8,128)}) fusion(f32[8,512,2048]{2,1,0:T(8,128)} %get-tuple-element.304, f32[8,512]{1,0:T(8,128)S(1)} %copy-done.69, bf16[512,8,64]{0,2,1:T(8,128)(2,1)S(1)} %bitcast.242, f32[2048,8,64]{0,2,1:T(8,128)S(1)} %bitcast.224, f32[8,64]{1,0:T(8,128)S(1)} %copy-done.89), kind=kOutput, calls=%fused_computation.5 | convolution fusion | flops 1101000704 | bytes 71862272 | tf_op jit(solution)/shard_map/while/body/eval_jaxpr/qhd,khd->hqk/dot_general | solution.py:112
  793.3 15.6 %convert_reduce_fusion.4 = (f32[8,64]{1,0:T(8,128)}, bf16[2048,8,64]{0,2,1:T(8,128)(2,1)}) fusion(f32[2048,8,64]{0,2,1:T(8,128)} %fusion.67, bf16[512,8,64]{0,2,1:T(8,128)(2,1)S(1)} %bitcast.243, f32[8,512,2048]{2,1,0:T(8,128)} %get-tuple-element.304, f32[8,512]{1,0:T(8,128)S(1)} %copy-done.69), kind=kOutput, calls=%fused_computation.98 | convolution fusion | flops 1094712832 | bytes 40388608 | tf_op jit(solution)/shard_map/while/body/eval_jaxpr/hqk,qhd->khd/dot_general | solution.py:110
  833.9 16.7 %multiply_convert_fusion.1 = bf16[8,512,1536]{2,1,0:T(8,128)(2,1)S(1)} fusion(f32[8,512,1536]{2,1,0:T(8,128)} %get-tuple-element.318, f32[8,512]{1,0:T(8,128)S(1)} %copy-done.80, f32[8,512,1536]{2,1,0:T(8,128)} %get-tuple-element.306, f32[8,512]{1,0:T(8,128)S(1)} %copy-done.73), kind=kLoop, calls=%fused_computation.9 | loop fusion | flops 31457280 | bytes 62947328 | tf_op jit(solution)/shard_map/while/body/eval_jaxpr/convert_element_type | solution.py:120
  864.8 28.0 %multiply_convert_fusion = bf16[8,512,2048]{2,1,0:T(8,128)(2,1)} fusion(f32[8,512,2048]{2,1,0:T(8,128)} %get-tuple-element.320, f32[8,512]{1,0:T(8,128)S(1)} %copy-done.79, f32[8,512,2048]{2,1,0:T(8,128)} %get-tuple-element.304, f32[8,512]{1,0:T(8,128)S(1)} %copy-done.69), kind=kLoop, calls=%fused_computation.4 | loop fusion | flops 41943040 | bytes 83918848 | tf_op jit(solution)/shard_map/while/body/eval_jaxpr/convert_element_type | solution.py:120
  955.6 14.0 convolution_convert_fusion.4
  978.8 15.6 %convolution_convert_fusion = bf16[1024,2048]{1,0:T(8,128)(2,1)} fusion(bf16[2048,2048]{1,0:T(8,128)(2,1)} %copy-done.106, f32[2048,1024]{1,0:T(8,128)} %copy-done, f32[1024]{0:T(1024)S(1)} %bitcast.297, f32[1024]{0:T(1024)S(1)} %bitcast.269, f32[2048]{0:T(1024)S(1)} %copy-done.58, f32[2048]{0:T(1024)S(1)} %copy-done.43), kind=kOutput, calls=%fused_computation.123 | convolution fusion | flops 8602517504 | bytes 20996096 | tf_op jit(solution)/shard_map/dot_general | solution.py:40
  1068.3 83.1 %all-reduce.19.cloned.1.call-done = bf16[3,1024,512]{2,0,1:T(4,128)(2,1)} async-done(((bf16[3,1024,512]{2,0,1:T(4,128)(2,1)}), bf16[3,1024,512]{2,0,1:T(4,128)(2,1)}) %all-reduce.19.cloned.1.call-update) | async-done | bytes 3145744
  1153.3 57.7 %reduce-scatter.4.cloned.1.call-done = bf16[512,64]{0,1:T(8,128)(2,1)} async-done(((bf16[512,1024]{0,1:T(8,128)(2,1)}), bf16[512,64]{0,1:T(8,128)(2,1)}) %reduce-scatter.4.cloned.1.call-update) | async-done | bytes 65552 | tf_op jit(solution)/shard_map/reduce_scatter | solution.py:273
  1212.4 74.2 %reduce-scatter.8.cloned.1.call-done = bf16[2048,64]{0,1:T(8,128)(2,1)} async-done(((bf16[2048,1024]{0,1:T(8,128)(2,1)}), bf16[2048,64]{0,1:T(8,128)(2,1)}) %reduce-scatter.8.cloned.1.call-update) | async-done | bytes 262160 | tf_op jit(solution)/shard_map/reduce_scatter | solution.py:279
  1288.4 73.9 %reduce-scatter.6.cloned.1.call-done = bf16[64,2048]{1,0:T(8,128)(2,1)} async-done(((bf16[1024,2048]{1,0:T(8,128)(2,1)}), bf16[64,2048]{1,0:T(8,128)(2,1)}) %reduce-scatter.6.cloned.1.call-update) | async-done | bytes 262160 | tf_op jit(solution)/shard_map/reduce_scatter | solution.py:276
  1364.1 128.0 %all-reduce.21.cloned.1.call-done = (f32[4,1024]{1,0:T(4,128)}, f32[4,1024]{1,0:T(4,128)}, f32[2,1024]{1,0:T(2,128)}, f32[2,1024]{1,0:T(2,128)}, f32[4096]{0:T(1024)}) async-done(((f32[4,1024]{1,0:T(4,128)}, f32[4,1024]{1,0:T(4,128)}, f32[2,1024]{1,0:T(2,128)}, f32[2,1024]{1,0:T(2,128)}, f32[4096]{0:T(1024)}), (f32[4,1024]{1,0:T(4,128)}, f32[4,1024]{1,0:T(4,128)}, f32[2,1024]{1,0:T(2,128)}, ...) | async-done | bytes 65552 | tf_op jit(solution)/shard_map/psum | solution.py:266
  (433 shorter events, 415.8 us)
Async XLA Ops:
  7.2 51.3 %all-gather.5.cloned.1.call-start = ((), (), s32[]{:S(2)}) async-start(), calls=%async_computation.3 | async-start | bytes 3342336 | tf_op jit(solution)/shard_map/all_gather | solution.py:156
  9.0 163.3 %all-gather.7.cloned.1.call-start = ((), (), s32[]{:S(2)}) async-start(), calls=%async_computation.4 | async-start | bytes 1114112 | tf_op jit(solution)/shard_map/all_gather | solution.py:157
  10.6 274.1 %all-reduce.11.cloned.1.call-start = ((), (), s32[]{:S(2)}) async-start(), calls=%async_computation.5 | async-start | bytes 8388608 | tf_op jit(solution)/shard_map/psum | solution.py:184
  14.2 132.7 %copy-start.88 = (f32[8,64]{1,0:T(8,128)}, f32[8,64]{1,0:T(8,128)S(1)}, u32[]{:S(2)}) copy-start(f32[8,64]{1,0:T(8,128)S(1)} %add.363) | copy-start | bytes 6148
  17.1 41.5 %copy-start.44 = (f32[2048]{0:T(1024)}, f32[2048]{0:T(1024)S(1)}, u32[]{:S(2)}) copy-start(f32[2048]{0:T(1024)S(1)} %broadcast_multiply_fusion.3) | copy-start | bytes 24580
  20.1 38.5 %copy-start.65 = (f32[2048]{0:T(1024)}, f32[2048]{0:T(1024)S(1)}, u32[]{:S(2)}) copy-start(f32[2048]{0:T(1024)S(1)} %fusion.108) | copy-start | bytes 24580
  21.3 47.6 %copy-start.94 = (f32[1,1024]{1,0:T(1,128)}, f32[1,1024]{1,0:T(1,128)S(1)}, u32[]{:S(2)}) copy-start(f32[1,1024]{1,0:T(1,128)S(1)} %get-tuple-element.292) | copy-start | bytes 12292
  69.3 59.4 %copy-start.12 = (bf16[1,2048,512]{1,2,0:T(8,128)(2,1)}, bf16[1,2048,512]{1,2,0:T(8,128)(2,1)S(1)}, u32[]{:S(2)}) copy-start(bf16[1,2048,512]{1,2,0:T(8,128)(2,1)S(1)} %slice.547) | copy-start | bytes 6291460
  102.3 60.6 %copy-start.74 = (f32[8,512]{1,0:T(8,128)}, f32[8,512]{1,0:T(8,128)S(1)}, u32[]{:S(2)}) copy-start(f32[8,512]{1,0:T(8,128)S(1)} %get-tuple-element.307) | copy-start | bytes 49156
  178.3 160.2 %all-gather.9.cloned.1.call-start = ((), (), s32[]{:S(2)}) async-start(), calls=%async_computation.6 | async-start | bytes 4456448 | tf_op jit(solution)/shard_map/all_gather | solution.py:158
  179.1 211.5 %all-gather.11.cloned.1.call-start = ((), (), s32[]{:S(2)}) async-start(), calls=%async_computation.7 | async-start | bytes 4456448 | tf_op jit(solution)/shard_map/all_gather | solution.py:159
  179.9 330.7 %all-reduce.13.cloned.1.call-start = ((), (), s32[]{:S(2)}) async-start(), calls=%async_computation.8 | async-start | bytes 8388608 | tf_op jit(solution)/shard_map/psum | solution.py:192
  296.7 41.8 %copy-start.59 = (f32[1,1024]{1,0:T(1,128)S(1)}, f32[1,1024]{1,0:T(1,128)}, u32[]{:S(2)}) copy-start(f32[1,1024]{1,0:T(1,128)} %get-tuple-element.289) | copy-start | bytes 12292
  296.7 41.8 %copy-start.92 = (f32[1,1024]{1,0:T(1,128)S(1)}, f32[1,1024]{1,0:T(1,128)}, u32[]{:S(2)}) copy-start(f32[1,1024]{1,0:T(1,128)} %get-tuple-element.293) | copy-start | bytes 12292
  296.7 391.8 %copy-start.42 = (f32[2048]{0:T(1024)}, f32[2048]{0:T(1024)S(1)}, u32[]{:S(2)}) copy-start(f32[2048]{0:T(1024)S(1)} %broadcast_multiply_fusion.1) | copy-start | bytes 24580
  301.0 387.5 %copy-start.57 = (f32[2048]{0:T(1024)}, f32[2048]{0:T(1024)S(1)}, u32[]{:S(2)}) copy-start(f32[2048]{0:T(1024)S(1)} %fusion.110) | copy-start | bytes 24580
  404.5 109.2 %copy-start.46 = (f32[1,1024]{1,0:T(1,128)S(1)}, f32[1,1024]{1,0:T(1,128)}, u32[]{:S(2)}) copy-start(f32[1,1024]{1,0:T(1,128)} %get-tuple-element.286) | copy-start | bytes 12292
  404.5 272.8 %all-reduce.15.cloned.1.call-start = ((), (), s32[]{:S(2)}) async-start(), calls=%async_computation.9 | async-start | bytes 8388608 | tf_op jit(solution)/shard_map/psum | solution.py:209
  569.2 468.0 %all-reduce.17.cloned.1.call-start = ((), (), s32[]{:S(2)}) async-start(), calls=%async_computation.10 | async-start | bytes 8388608 | tf_op jit(solution)/shard_map/psum | solution.py:244
  929.2 222.2 %all-reduce.19.cloned.1.call-start = ((), (), s32[]{:S(2)}) async-start(), calls=%async_computation.14 | async-start | bytes 8388608
  949.7 261.2 %reduce-scatter.4.cloned.1.call-start = ((), (), s32[]{:S(2)}) async-start(), calls=%async_computation.11 | async-start | bytes 1114112 | tf_op jit(solution)/shard_map/reduce_scatter | solution.py:273
  955.4 331.2 %reduce-scatter.8.cloned.1.call-start = ((), (), s32[]{:S(2)}) async-start(), calls=%async_computation.13 | async-start | bytes 4456448 | tf_op jit(solution)/shard_map/reduce_scatter | solution.py:279
  969.6 392.7 %reduce-scatter.6.cloned.1.call-start = ((), (), s32[]{:S(2)}) async-start(), calls=%async_computation.12 | async-start | bytes 4456448 | tf_op jit(solution)/shard_map/reduce_scatter | solution.py:276
  994.5 497.6 %all-reduce.21.cloned.1.call-start = ((), (), s32[]{:S(2)}) async-start(), calls=%async_computation.15 | async-start | bytes 131072 | tf_op jit(solution)/shard_map/psum | solution.py:266
  (115 other events, 1093.5 us)
Sparse Core Ops, SparseCore 0:
  10.8 47.6 all-gather.4
  61.3 36.7 all-gather.6
  178.4 106.2 all-reduce.10
  287.5 50.9 all-gather.8
  341.3 49.2 all-gather.10
  404.6 105.9 all-reduce.12
  569.4 107.8 all-reduce.14
  929.3 107.8 all-reduce.16
  1040.9 110.4 all-reduce.18
  1155.3 55.5 reduce-scatter.3
  1214.8 71.7 reduce-scatter.7
  1290.8 71.4 reduce-scatter.5
  1369.9 122.1 all-reduce.20
where the time goes:
time: 1510 us
  waiting for transfers between devices  846 us (56%)
  matrix products  371 us (25%)
  other arithmetic  211 us (14%)
  local copies, waits for them, and re-layouts  59.2 us (4%)
  between operations  16.5 us (1%)
    psum x1, waiting for transfers between devices, per_device(): lax.psum((gain_terms, shift_terms, head_full, bias_terms, hidden_full), (...  128 us
    psum x1, waiting for transfers between devices, per_device(): lax.psum(partial_mid.astype(jnp.bfloat16), 'tensor').astype(jnp.float32)  108 us
    psum x1, waiting for transfers between devices, per_device(): lax.psum(partial_mlp.astype(jnp.bfloat16), 'tensor').astype(jnp.float32)  106 us
    psum x1, waiting for transfers between devices, per_device(): lax.psum(partial_attn.astype(jnp.bfloat16), 'tensor').astype(jnp.float32)  105 us
    unnamed x14, waiting for transfers between devices  83.3 us
    reduce_scatter x1, waiting for transfers between devices, per_device(): lax.psum_scatter(grad_down.astype(jnp.bfloat16), 'dp', scatter_dimension=...  74.2 us
    reduce_scatter x1, waiting for transfers between devices, per_device(): lax.psum_scatter(grad_up.astype(jnp.bfloat16), 'dp', scatter_dimension=0,...  73.9 us
    convert_element_type x4, other arithmetic, attend_backward(): d_scores = d_scores.astype(jnp.bfloat16)  63.3 us
  transfers between devices with their start and end apart: 13, of which 12 were waited for; matrix products, arithmetic and copies ran while one was open for 20% of the time, Pallas kernels for 0%

commit v1 on v0

--- a/solution.py
+++ b/solution.py
@@ -206,7 +206,9 @@
     grad_up = contract_rows(normed_mid, d_pre)
     grad_hidden = jnp.sum(d_pre, axis=0, dtype=jnp.float32)
     partial_mid = contract_cols(d_pre, w_up)
-    d_mid = lax.psum(partial_mid.astype(jnp.bfloat16), "tensor").astype(jnp.float32)
+    d_mid = jnp.sum(lax.all_gather(partial_mid.astype(jnp.bfloat16), "tensor"), axis=0).astype(
+        jnp.float32
+    )
     d_resid_part, gain_two, shift_two = norm_back(
         resid, norm_gain[2], norm_bias[2], d_mid, row_start, shard_rows
     )

time: 1510 us -> 1390 us (0.921)
  waiting for transfers between devices: 846 us -> 688 us
  other arithmetic: 211 us -> 227 us
    psum x1 -> x0, waiting for transfers between devices: 108 us -> none  [per_device(): lax.psum(partial_mid.astype(jnp.bfloat16), 'tensor').astype(jnp.float32)]
    reduce_scatter x1, waiting for transfers between devices: 74.2 us -> 0.02 us  [per_device(): lax.psum_scatter(grad_down.astype(jnp.bfloat16), 'dp', scatter_dimension=...]
    reduce_scatter x1, waiting for transfers between devices: 73.9 us -> 0.01 us  [per_device(): lax.psum_scatter(grad_up.astype(jnp.bfloat16), 'dp', scatter_dimension=0,...]
    all_gather x0 -> x1, waiting for transfers between devices: none -> 72.9 us  [per_device(): lax.all_gather(partial_mid.astype(jnp.bfloat16), 'tensor')]
    psum x1, waiting for transfers between devices: 9.03 us -> 33.6 us  [per_device(): lax.psum(partial_in.astype(jnp.bfloat16), 'tensor').astype(jnp.float32)]
    unnamed x257 -> x267, local copies, waits for them, and re-layouts: 24.3 us -> 31.9 us
  transfers between devices with their start and end apart: 13 -> 13, of which waited for: 12 -> 10; matrix products, arithmetic and copies ran while one was open for 20% -> 41% of each run, Pallas kernels for 0% -> 0%
where the time goes in v1:
time: 1390 us; the launch traced here: 1380 us
  waiting for transfers between devices  688 us (49%)
  matrix products  379 us (27%)
  other arithmetic  227 us (16%)
  local copies, waits for them, and re-layouts  69.5 us (5%)
  between operations  16.7 us (1%)
    psum x1, waiting for transfers between devices, per_device(): lax.psum((gain_terms, shift_terms, head_full, bias_terms, hidden_full), (...  130 us
    psum x1, waiting for transfers between devices, per_device(): lax.psum(partial_mlp.astype(jnp.bfloat16), 'tensor').astype(jnp.float32)  106 us
    psum x1, waiting for transfers between devices, per_device(): lax.psum(partial_attn.astype(jnp.bfloat16), 'tensor').astype(jnp.float32)  105 us
    unnamed x14, waiting for transfers between devices  83.8 us
    all_gather x1, waiting for transfers between devices, per_device(): lax.all_gather(partial_mid.astype(jnp.bfloat16), 'tensor')  72.9 us
    convert_element_type x4, other arithmetic, attend_backward(): d_scores = d_scores.astype(jnp.bfloat16)  63.5 us
    reduce_scatter x1, waiting for transfers between devices, per_device(): lax.psum_scatter(grad_proj.astype(jnp.bfloat16), 'dp', scatter_dimension=...  57.2 us
    dot_general x4, matrix products, attend_backward(): jnp.einsum('qhd,khd->hqk', block_grad, values[:row_last], preferred_eleme...  53.7 us
  transfers between devices with their start and end apart: 13, of which 10 were waited for; matrix products, arithmetic and copies ran while one was open for 41% of the time, Pallas kernels for 0%

profile of v1, /device:TPU:1, one launch (start us, length us, event | category | flops | bytes accessed | tf_op | source)
XLA Modules:
  0.0 1381.5 jit_solution(6354189971836202565)
XLA Ops:
  26.8 31.8 %all-gather.7.cloned.1.call-done = bf16[3,1024,512]{2,1,0:T(8,128)(2,1)} async-done(((bf16[3,64,512]{2,1,0:T(8,128)(2,1)}), bf16[3,1024,512]{2,1,0:T(8,128)(2,1)}) %all-gather.7.cloned.1.call-update) | async-done | bytes 3145744 | tf_op jit(solution)/shard_map/all_gather | solution.py:156
  102.4 14.9 %fusion.134 = (f32[8,512]{1,0:T(8,128)S(1)}, f32[8,512,1536]{2,1,0:T(8,128)}) fusion(pred[512,1536]{1,0:T(8,128)(4,1)} %fusion.71, bf16[512,8,64]{0,2,1:T(8,128)(2,1)} %bitcast.234, bf16[1536,8,64]{0,2,1:T(8,128)(2,1)} %bitcast.213), kind=kOutput, calls=%fused_computation.237 | convolution fusion | flops 830473728 | bytes 28065792 | tf_op jit(solution)/shard_map/while/body/eval_jaxpr/sub | solution.py:73
  128.9 18.2 %fusion.133 = (f32[8,512]{1,0:T(8,128)S(1)}, f32[8,512,2048]{2,1,0:T(8,128)}) fusion(pred[512,2048]{1,0:T(8,128)(4,1)} %fusion.53, bf16[512,8,64]{0,2,1:T(8,128)(2,1)S(1)} %bitcast.232, bf16[2048,8,64]{0,2,1:T(8,128)(2,1)S(1)} %bitcast.205), kind=kOutput, calls=%fused_computation.236 | convolution fusion | flops 1107298304 | bytes 37240832 | tf_op jit(solution)/shard_map/while/body/eval_jaxpr/sub | solution.py:73
  147.1 15.9 %fusion.99 = bf16[8,64,512]{2,1,0:T(8,128)(2,1)} fusion(f32[2048,8,64]{0,2,1:T(8,128)} %bitcast.225, f32[8,64]{1,0:T(8,128)S(1)} %add.361, f32[8,512,2048]{2,1,0:T(8,128)} %get-tuple-element.304, f32[8,512]{1,0:T(8,128)S(1)} %get-tuple-element.303), kind=kOutput, calls=%fused_computation.170 | convolution fusion | flops 1092878336 | bytes 38291456 | tf_op jit(solution)/shard_map/while/body/eval_jaxpr/hqk,khd->qhd/dot_general | solution.py:77
  180.2 104.7 %all-reduce.10.cloned.1.call-done = bf16[2048,1024]{1,0:T(8,128)(2,1)} async-done(((bf16[2048,1024]{1,0:T(8,128)(2,1)}), bf16[2048,1024]{1,0:T(8,128)(2,1)}) %all-reduce.10.cloned.1.call-update) | async-done | bytes 4194320 | tf_op jit(solution)/shard_map/psum | solution.py:184
  301.8 37.0 %all-gather.11.cloned.1.call-done = bf16[1024,2048]{1,0:T(8,128)(2,1)} async-done(((bf16[64,2048]{1,0:T(8,128)(2,1)}), bf16[1024,2048]{1,0:T(8,128)(2,1)}) %all-gather.11.cloned.1.call-update) | async-done | bytes 4194320 | tf_op jit(solution)/shard_map/all_gather | solution.py:158
  338.9 20.4 %multiply_convert_fusion.3 = (bf16[2048,2048]{1,0:T(8,128)(2,1)}, f32[2048,2048]{1,0:T(8,128)}) fusion(f32[2048]{0:T(1024)S(1)} %dynamic_slice.68, bf16[1024,2048]{1,0:T(8,128)(2,1)} %all-gather.11.cloned.1.call-done, f32[2048,1024]{1,0:T(8,128)} %copy-done, f32[1024]{0:T(1024)S(1)} %bitcast.300, f32[1024]{0:T(1024)S(1)} %bitcast.270, ...), kind=kOutput, calls=%fused_computation.26 | convolution fusion | flops 8642363392 | bytes 37781504 | tf_op jit(solution)/shard_map/dot_general | solution.py:188
  359.2 31.7 %all-gather.13.cloned.1.call-done = bf16[2048,1024]{0,1:T(8,128)(2,1)} async-done(((bf16[2048,64]{0,1:T(8,128)(2,1)}), bf16[2048,1024]{0,1:T(8,128)(2,1)}) %all-gather.13.cloned.1.call-update) | async-done | bytes 4194320 | tf_op jit(solution)/shard_map/all_gather | solution.py:159
  390.9 13.9 %convolution_convert_fusion.2 = bf16[2048,1024]{1,0:T(8,128)(2,1)} fusion(bf16[2048,2048]{1,0:T(8,128)(2,1)} %get-tuple-element.311, bf16[2048,1024]{0,1:T(8,128)(2,1)} %all-gather.13.cloned.1.call-done), kind=kOutput, calls=%fused_computation.125 | convolution fusion | flops 8592031744 | bytes 16777216 | tf_op jit(solution)/shard_map/dot_general | solution.py:190
  405.0 105.9 %all-reduce.12.cloned.1.call-done = bf16[2048,1024]{1,0:T(8,128)(2,1)} async-done(((bf16[2048,1024]{1,0:T(8,128)(2,1)}), bf16[2048,1024]{1,0:T(8,128)(2,1)}) %all-reduce.12.cloned.1.call-update) | async-done | bytes 4194320 | tf_op jit(solution)/shard_map/psum | solution.py:192
  531.3 24.9 %convert_reduce_fusion = (f32[2048]{0:T(1024)}, bf16[2048,2048]{1,0:T(8,128)(2,1)S(1)}) fusion(f32[2048,2048]{1,0:T(8,128)} %get-tuple-element.312, f32[2048]{0:T(1024)S(1)} %dynamic_slice.68, bf16[2048,1024]{1,0:T(8,128)(2,1)S(1)} %get-tuple-element.273, bf16[2048,1024]{0,1:T(8,128)(2,1)S(1)} %copy-done.103), kind=kOutput, calls=%fused_computation.23 | convolution fusion | flops 8686401536 | bytes 33570816 | tf_op jit(solution)/shard_map/dot_general | solution.py:46
  570.3 14.0 %convolution_convert_fusion.4 = bf16[2048,1024]{0,1:T(8,128)(2,1)} fusion(bf16[2048,2048]{1,0:T(8,128)(2,1)} %get-tuple-element.311, bf16[2048,1024]{1,0:T(8,128)(2,1)} %copy-done.17), kind=kOutput, calls=%fused_computation.127 | convolution fusion | flops 8592031744 | bytes 16777216 | tf_op jit(solution)/shard_map/dot_general | solution.py:40
  584.3 17.1 %convolution_convert_fusion = bf16[1024,2048]{1,0:T(8,128)(2,1)} fusion(bf16[2048,2048]{1,0:T(8,128)(2,1)} %copy-done.109, f32[2048,1024]{1,0:T(8,128)} %copy-done, f32[1024]{0:T(1024)S(1)} %bitcast.301, f32[1024]{0:T(1024)S(1)} %bitcast.271, f32[2048]{0:T(1024)S(1)} %fusion.110, f32[2048]{0:T(1024)S(1)} %broadcast_multiply_fusion.1), kind=kOutput, calls=%fused_computation.123 | convolution fusion | flops 8602517504 | bytes 20996096 | tf_op jit(solution)/shard_map/dot_general | solution.py:40
  601.5 72.9 %all-gather.15.cloned.1.call-done = bf16[4096,1024]{1,0:T(8,128)(2,1)} async-done(((bf16[2048,1024]{1,0:T(8,128)(2,1)}), bf16[4096,1024]{1,0:T(8,128)(2,1)}) %all-gather.15.cloned.1.call-update) | async-done | bytes 8388624 | tf_op jit(solution)/shard_map/all_gather | solution.py:209
  750.2 17.3 %multiply_reduce_fusion.1 = (f32[8,512]{1,0:T(8,128)}, f32[8,512,1536]{2,1,0:T(8,128)}) fusion(f32[8,512,1536]{2,1,0:T(8,128)} %get-tuple-element.306, f32[8,512]{1,0:T(8,128)S(1)} %copy-done.78, bf16[512,8,64]{0,2,1:T(8,128)(2,1)S(1)} %bitcast.246, bf16[1536,8,64]{0,2,1:T(8,128)(2,1)S(1)} %bitcast.239), kind=kOutput, calls=%fused_computation.10 | convolution fusion | flops 824176640 | bytes 52461568 | tf_op jit(solution)/shard_map/while/body/eval_jaxpr/qhd,khd->hqk/dot_general | solution.py:112
  767.6 13.7 fusion.67
  781.3 22.6 %multiply_reduce_fusion = (f32[8,512]{1,0:T(8,128)}, f32[8,512,2048]{2,1,0:T(8,128)}) fusion(f32[8,512,2048]{2,1,0:T(8,128)} %get-tuple-element.304, f32[8,512]{1,0:T(8,128)S(1)} %copy-done.76, bf16[512,8,64]{0,2,1:T(8,128)(2,1)S(1)} %bitcast.244, f32[2048,8,64]{0,2,1:T(8,128)S(1)} %bitcast.226, f32[8,64]{1,0:T(8,128)S(1)} %copy-done.96), kind=kOutput, calls=%fused_computation.5 | convolution fusion | flops 1101000704 | bytes 71862272 | tf_op jit(solution)/shard_map/while/body/eval_jaxpr/qhd,khd->hqk/dot_general | solution.py:112
  803.9 15.8 %convert_reduce_fusion.4 = (f32[8,64]{1,0:T(8,128)}, bf16[2048,8,64]{0,2,1:T(8,128)(2,1)}) fusion(f32[2048,8,64]{0,2,1:T(8,128)} %fusion.67, bf16[512,8,64]{0,2,1:T(8,128)(2,1)S(1)} %bitcast.245, f32[8,512,2048]{2,1,0:T(8,128)} %get-tuple-element.304, f32[8,512]{1,0:T(8,128)S(1)} %copy-done.76), kind=kOutput, calls=%fused_computation.98 | convolution fusion | flops 1094712832 | bytes 40388608 | tf_op jit(solution)/shard_map/while/body/eval_jaxpr/hqk,qhd->khd/dot_general | solution.py:110
  846.4 16.7 %multiply_convert_fusion.1 = bf16[8,512,1536]{2,1,0:T(8,128)(2,1)S(1)} fusion(f32[8,512,1536]{2,1,0:T(8,128)} %get-tuple-element.318, f32[8,512]{1,0:T(8,128)S(1)} %copy-done.88, f32[8,512,1536]{2,1,0:T(8,128)} %get-tuple-element.306, f32[8,512]{1,0:T(8,128)S(1)} %copy-done.80), kind=kLoop, calls=%fused_computation.9 | loop fusion | flops 31457280 | bytes 62947328 | tf_op jit(solution)/shard_map/while/body/eval_jaxpr/convert_element_type | solution.py:120
  875.8 27.8 %multiply_convert_fusion = bf16[8,512,2048]{2,1,0:T(8,128)(2,1)} fusion(f32[8,512,2048]{2,1,0:T(8,128)} %get-tuple-element.320, f32[8,512]{1,0:T(8,128)S(1)} %copy-done.86, f32[8,512,2048]{2,1,0:T(8,128)} %get-tuple-element.304, f32[8,512]{1,0:T(8,128)S(1)} %copy-done.76), kind=kLoop, calls=%fused_computation.4 | loop fusion | flops 41943040 | bytes 83918848 | tf_op jit(solution)/shard_map/while/body/eval_jaxpr/convert_element_type | solution.py:120
  1029.6 33.6 %all-reduce.14.cloned.1.call-done = bf16[2048,1024]{1,0:T(8,128)(2,1)} async-done(((bf16[2048,1024]{1,0:T(8,128)(2,1)}), bf16[2048,1024]{1,0:T(8,128)(2,1)}) %all-reduce.14.cloned.1.call-update) | async-done | bytes 4194320 | tf_op jit(solution)/shard_map/psum | solution.py:246
  1094.3 83.5 %all-reduce.16.cloned.1.call-done = bf16[3,1024,512]{2,0,1:T(4,128)(2,1)} async-done(((bf16[3,1024,512]{2,0,1:T(4,128)(2,1)}), bf16[3,1024,512]{2,0,1:T(4,128)(2,1)}) %all-reduce.16.cloned.1.call-update) | async-done | bytes 3145744
  1179.7 57.2 %reduce-scatter.4.cloned.1.call-done = bf16[512,64]{0,1:T(8,128)(2,1)} async-done(((bf16[512,1024]{0,1:T(8,128)(2,1)}), bf16[512,64]{0,1:T(8,128)(2,1)}) %reduce-scatter.4.cloned.1.call-update) | async-done | bytes 65552 | tf_op jit(solution)/shard_map/reduce_scatter | solution.py:275
  1238.4 129.5 %all-reduce.18.cloned.1.call-done = (f32[4,1024]{1,0:T(4,128)}, f32[4,1024]{1,0:T(4,128)}, f32[2,1024]{1,0:T(2,128)}, f32[2,1024]{1,0:T(2,128)}, f32[4096]{0:T(1024)}) async-done(((f32[4,1024]{1,0:T(4,128)}, f32[4,1024]{1,0:T(4,128)}, f32[2,1024]{1,0:T(2,128)}, f32[2,1024]{1,0:T(2,128)}, f32[4096]{0:T(1024)}), (f32[4,1024]{1,0:T(4,128)}, f32[4,1024]{1,0:T(4,128)}, f32[2,1024]{1,0:T(2,128)}, ...) | async-done | bytes 65552 | tf_op jit(solution)/shard_map/psum | solution.py:268
  (444 shorter events, 423.9 us)
Async XLA Ops:
  7.2 51.3 %all-gather.7.cloned.1.call-start = ((), (), s32[]{:S(2)}) async-start(), calls=%async_computation.3 | async-start | bytes 3342336 | tf_op jit(solution)/shard_map/all_gather | solution.py:156
  9.0 163.5 %all-gather.9.cloned.1.call-start = ((), (), s32[]{:S(2)}) async-start(), calls=%async_computation.4 | async-start | bytes 1114112 | tf_op jit(solution)/shard_map/all_gather | solution.py:157
  10.6 274.3 %all-reduce.10.cloned.1.call-start = ((), (), s32[]{:S(2)}) async-start(), calls=%async_computation.5 | async-start | bytes 8388608 | tf_op jit(solution)/shard_map/psum | solution.py:184
  14.2 132.9 %copy-start.95 = (f32[8,64]{1,0:T(8,128)}, f32[8,64]{1,0:T(8,128)S(1)}, u32[]{:S(2)}) copy-start(f32[8,64]{1,0:T(8,128)S(1)} %add.361) | copy-start | bytes 6148
  17.1 41.5 %copy-start.51 = (f32[2048]{0:T(1024)}, f32[2048]{0:T(1024)S(1)}, u32[]{:S(2)}) copy-start(f32[2048]{0:T(1024)S(1)} %broadcast_multiply_fusion.3) | copy-start | bytes 24580
  21.3 47.6 %copy-start.99 = (f32[1,1024]{1,0:T(1,128)}, f32[1,1024]{1,0:T(1,128)S(1)}, u32[]{:S(2)}) copy-start(f32[1,1024]{1,0:T(1,128)S(1)} %get-tuple-element.292) | copy-start | bytes 12292
  69.3 59.6 %copy-start.15 = (bf16[1,2048,512]{1,2,0:T(8,128)(2,1)}, bf16[1,2048,512]{1,2,0:T(8,128)(2,1)S(1)}, u32[]{:S(2)}) copy-start(bf16[1,2048,512]{1,2,0:T(8,128)(2,1)S(1)} %slice.547) | copy-start | bytes 6291460
  102.4 60.6 %copy-start.81 = (f32[8,512]{1,0:T(8,128)}, f32[8,512]{1,0:T(8,128)S(1)}, u32[]{:S(2)}) copy-start(f32[8,512]{1,0:T(8,128)S(1)} %get-tuple-element.307) | copy-start | bytes 49156
  178.4 160.4 %all-gather.11.cloned.1.call-start = ((), (), s32[]{:S(2)}) async-start(), calls=%async_computation.6 | async-start | bytes 4456448 | tf_op jit(solution)/shard_map/all_gather | solution.py:158
  179.2 211.7 %all-gather.13.cloned.1.call-start = ((), (), s32[]{:S(2)}) async-start(), calls=%async_computation.7 | async-start | bytes 4456448 | tf_op jit(solution)/shard_map/all_gather | solution.py:159
  180.1 330.9 %all-reduce.12.cloned.1.call-start = ((), (), s32[]{:S(2)}) async-start(), calls=%async_computation.8 | async-start | bytes 8388608 | tf_op jit(solution)/shard_map/psum | solution.py:192
  180.2 113.0 %copy-start.49 = (f32[1,1024]{1,0:T(1,128)}, f32[1,1024]{1,0:T(1,128)S(1)}, u32[]{:S(2)}) copy-start(f32[1,1024]{1,0:T(1,128)S(1)} %get-tuple-element.296) | copy-start | bytes 12292
  296.9 42.0 %copy-start.68 = (f32[1,1024]{1,0:T(1,128)S(1)}, f32[1,1024]{1,0:T(1,128)}, u32[]{:S(2)}) copy-start(f32[1,1024]{1,0:T(1,128)} %get-tuple-element.289) | copy-start | bytes 12292
  296.9 42.0 %copy-start.101 = (f32[1,1024]{1,0:T(1,128)S(1)}, f32[1,1024]{1,0:T(1,128)}, u32[]{:S(2)}) copy-start(f32[1,1024]{1,0:T(1,128)} %get-tuple-element.293) | copy-start | bytes 12292
  404.8 109.2 %copy-start.53 = (f32[1,1024]{1,0:T(1,128)S(1)}, f32[1,1024]{1,0:T(1,128)}, u32[]{:S(2)}) copy-start(f32[1,1024]{1,0:T(1,128)} %get-tuple-element.286) | copy-start | bytes 12292
  404.8 269.6 %all-gather.15.cloned.1.call-start = ((), (), s32[]{:S(2)}) async-start(), calls=%async_computation.13 | async-start | bytes 12582912 | tf_op jit(solution)/shard_map/all_gather | solution.py:209
  570.2 439.8 %reduce-scatter.8.cloned.1.call-start = ((), (), s32[]{:S(2)}) async-start(), calls=%async_computation.12 | async-start | bytes 4456448 | tf_op jit(solution)/shard_map/reduce_scatter | solution.py:281
  584.3 427.6 %reduce-scatter.6.cloned.1.call-start = ((), (), s32[]{:S(2)}) async-start(), calls=%async_computation.11 | async-start | bytes 4456448 | tf_op jit(solution)/shard_map/reduce_scatter | solution.py:278
  601.5 461.7 %all-reduce.14.cloned.1.call-start = ((), (), s32[]{:S(2)}) async-start(), calls=%async_computation.9 | async-start | bytes 8388608 | tf_op jit(solution)/shard_map/psum | solution.py:246
  954.9 222.9 %all-reduce.16.cloned.1.call-start = ((), (), s32[]{:S(2)}) async-start(), calls=%async_computation.14 | async-start | bytes 8388608
  1001.7 235.2 %reduce-scatter.4.cloned.1.call-start = ((), (), s32[]{:S(2)}) async-start(), calls=%async_computation.10 | async-start | bytes 1114112 | tf_op jit(solution)/shard_map/reduce_scatter | solution.py:275
  1028.5 39.3 %copy-start.61 = (f32[2048]{0:T(1024)S(1)}, f32[2048]{0:T(1024)}, u32[]{:S(2)}) copy-start(f32[2048]{0:T(1024)} %copy-done.60) | copy-start | bytes 24580
  1028.5 339.4 %all-reduce.18.cloned.1.call-start = ((), (), s32[]{:S(2)}) async-start(), calls=%async_computation.15 | async-start | bytes 131072 | tf_op jit(solution)/shard_map/psum | solution.py:268
  1029.6 45.1 %copy-start.74 = (f32[2,1024]{1,0:T(2,128)}, f32[2,1024]{1,0:T(2,128)S(1)}, u32[]{:S(2)}) copy-start(f32[2,1024]{1,0:T(2,128)S(1)} %constant_dynamic-update-slice_fusion) | copy-start | bytes 24580
  (120 other events, 1169.6 us)
Sparse Core Ops, SparseCore 0:
  10.8 47.6 all-gather.6
  61.3 36.7 all-gather.8
  178.6 106.2 all-reduce.9
  287.7 51.1 all-gather.10
  341.7 49.2 all-gather.12
  404.9 105.9 all-reduce.11
  570.3 103.9 all-gather.14
  678.2 70.5 reduce-scatter.7
  753.2 72.0 reduce-scatter.5
  955.0 108.1 all-reduce.13
  1067.3 110.4 all-reduce.15
  1181.3 55.5 reduce-scatter.3
  1245.6 122.2 all-reduce.17
